TPU v7x, 32 devices: a whole 2x2x4 slice. The times are simulated.
32 devices in a mesh: items: 16 (over z, y, core), seq: 2 (over x).
Axes of the slice: x: 2, y: 2, z: 4, core: 2. Of those that a mesh axis runs over, the one named last changes fastest.
Arguments:
- tokens: bfloat16 [16, 1280, 1024], P('items', 'seq'), may hold values from -6 to 6
- cotangent: bfloat16 [16, 1280, 1024], P('items', 'seq'), may hold values from -6 to 6
- prompt_len: int32 [16], P('items'), may hold values from 150 to 600
- section_ids: int32 [16], P('items'), may hold values from 0 to 7
- section_table: bfloat16 [8, 1024], replicated, may hold values from -6 to 6
- w_query: bfloat16 [1024, 1024], P('items'), may hold values from -0.1875 to 0.1875
- w_key: bfloat16 [1024, 1024], P('items'), may hold values from -0.1875 to 0.1875
- w_value: bfloat16 [1024, 1024], P('items'), may hold values from -0.1875 to 0.1875
- w_out: bfloat16 [1024, 1024], P('items'), may hold values from -4 to 4
- w_up: bfloat16 [1024, 4096], P('items'), may hold values from -0.1875 to 0.1875
- w_down: bfloat16 [4096, 1024], P('items'), may hold values from -0.09375 to 0.09375
- w_ada_one: bfloat16 [1024, 2048], P('items'), may hold values from -0.09375 to 0.09375
- w_ada_two: bfloat16 [1024, 2048], P('items'), may hold values from -0.09375 to 0.09375
Outputs:
- layer_out: bfloat16 [16, 1280, 1024], P('items', 'seq')
- input_grad: float32 [16, 1280, 1024], P('items', 'seq')
- grad_query: float32 [1024, 1024], P(('items', 'seq'))
- grad_key: float32 [1024, 1024], P(('items', 'seq'))
- grad_value: float32 [1024, 1024], P(('items', 'seq'))
- grad_out: float32 [1024, 1024], P(('items', 'seq'))
- grad_up: float32 [1024, 4096], P(('items', 'seq'))
- grad_down: float32 [4096, 1024], P(('items', 'seq'))
- grad_ada_one: float32 [1024, 2048], P(('items', 'seq'))
- grad_ada_two: float32 [1024, 2048], P(('items', 'seq'))
- grad_table: float32 [8, 1024], P(None, ('items', 'seq'))
Inputs may be any that keep to these rules, and one draw needn't show every extreme that they name: `prompt_len`: prompt frames at and past an item's length are padding. `section_ids`: the number of items per section is uneven across sections.
All inputs are finite; a program needn't handle non-finite values.
Results may differ from a plain program's by a relative error of at most 0.019.
Values may be sent and summed in bfloat16 or wider, within the bound.
No kernel may reach another device: no remote copies, remote signals or barrier semaphores. Data moves between devices by JAX's collectives and lax.ppermute only.
A program may use at most 384 MiB of HBM per device.

v0:
```python
from functools import partial
import math
import jax
import jax.numpy as jnp
from jax import lax
from jax.sharding import PartitionSpec as P

HEADS = 16
HEAD_DIM = 64
PROMPT = 640
EPSILON = 1e-05
MASKED = -1e30


def exact(left, right):
    return jnp.dot(left, right, precision=lax.Precision.HIGHEST)


def dot_rows(left, right):
    return lax.dot_general(
        left, right, (((0,), (0,)), ((), ())), preferred_element_type=jnp.float32
    )


def dot_last(left, right):
    return lax.dot_general(
        left, right, (((1,), (1,)), ((), ())), preferred_element_type=jnp.float32
    )


def ada_norm(values, ada):
    width = values.shape[-1]
    centred = values - jnp.mean(values, axis=-1, keepdims=True)
    spread = jnp.mean(centred * centred, axis=-1, keepdims=True)
    normed = centred * lax.rsqrt(spread + EPSILON)
    return (1.0 + ada[:, None, :width]) * normed + ada[:, None, width:]


def split_heads(block):
    return block.reshape(block.shape[0], HEADS, HEAD_DIM)


def frames_major(grad, dim, items_count, seq_count):
    shape = grad.shape
    piece = shape[dim] // (items_count * seq_count)
    parted = grad.reshape(shape[:dim] + (items_count, seq_count, piece) + shape[dim + 1 :])
    return jnp.swapaxes(parted, dim, dim + 1).reshape(shape)


def shards(
    tokens,
    cotangent,
    prompt_len,
    section_ids,
    section_table,
    w_query,
    w_key,
    w_value,
    w_out,
    w_up,
    w_down,
    w_ada_one,
    w_ada_two,
):
    full_query, full_key, full_value, full_out, full_up, full_down, full_ada_one, full_ada_two = (
        lax.all_gather(w_query, "items", axis=0, tiled=True),
        lax.all_gather(w_key, "items", axis=0, tiled=True),
        lax.all_gather(w_value, "items", axis=0, tiled=True),
        lax.all_gather(w_out, "items", axis=0, tiled=True),
        lax.all_gather(w_up, "items", axis=0, tiled=True),
        lax.all_gather(w_down, "items", axis=0, tiled=True),
        lax.all_gather(w_ada_one, "items", axis=0, tiled=True),
        lax.all_gather(w_ada_two, "items", axis=0, tiled=True),
    )
    batch, rows, width = tokens.shape
    items_count = lax.axis_size("items")
    seq_count = lax.axis_size("seq")
    frames_all = rows * seq_count
    scale = 1.0 / math.sqrt(HEAD_DIM)
    position = lax.axis_index("seq") * rows + jnp.arange(rows)
    key_place = jnp.arange(frames_all)
    inputs = tokens.astype(jnp.float32)
    choose = (section_ids[:, None] == jnp.arange(section_table.shape[0])[None, :]).astype(
        jnp.float32
    )
    cond = exact(choose, section_table.astype(jnp.float32))
    ada_one_w = full_ada_one.astype(jnp.float32)
    ada_two_w = full_ada_two.astype(jnp.float32)
    ada_one = exact(cond, ada_one_w)
    ada_two = exact(cond, ada_two_w)
    normed_one, back_one = jax.vjp(ada_norm, inputs, ada_one)
    low_one = normed_one.astype(jnp.bfloat16).reshape(-1, width)
    query = (
        jnp.dot(low_one, full_query, preferred_element_type=jnp.float32)
        .astype(jnp.bfloat16)
        .reshape(batch, rows, width)
    )
    keys_here = (
        jnp.dot(low_one, full_key, preferred_element_type=jnp.float32)
        .astype(jnp.bfloat16)
        .reshape(batch, rows, width)
    )
    values_here = (
        jnp.dot(low_one, full_value, preferred_element_type=jnp.float32)
        .astype(jnp.bfloat16)
        .reshape(batch, rows, width)
    )
    keys_all, values_all = (
        lax.all_gather(keys_here, "seq", axis=1, tiled=True),
        lax.all_gather(values_here, "seq", axis=1, tiled=True),
    )

    def masked_scores(query_item, keys_item, length, query_place, key_spot):
        raw = (
            jnp.einsum(
                "qhd,khd->hqk",
                split_heads(query_item),
                split_heads(keys_item),
                preferred_element_type=jnp.float32,
            )
            * scale
        )
        allowed = (key_spot[None, :] < length) | (key_spot[None, :] >= PROMPT) & (
            query_place[:, None] >= PROMPT
        )
        return jnp.where(allowed[None], raw, MASKED)

    def attend(packed):
        query_item, keys_item, values_item, length = packed
        scores = masked_scores(query_item, keys_item, length, position, key_place)
        peak = jnp.max(scores, axis=-1, keepdims=True)
        expo = jnp.exp(scores - peak)
        total = jnp.sum(expo, axis=-1, keepdims=True)
        probs = (expo / total).astype(jnp.bfloat16)
        mixed_item = jnp.einsum(
            "hqk,khd->qhd", probs, split_heads(values_item), preferred_element_type=jnp.float32
        )
        return (
            mixed_item.astype(jnp.bfloat16).reshape(rows, width),
            (peak + jnp.log(total))[..., 0],
        )

    mixed, log_total = lax.map(attend, (query, keys_all, values_all, prompt_len))
    mixed_flat = mixed.reshape(-1, width)
    attended = inputs + jnp.dot(mixed_flat, full_out, preferred_element_type=jnp.float32).reshape(
        batch, rows, width
    )
    normed_two, back_two = jax.vjp(ada_norm, attended, ada_two)
    low_two = normed_two.astype(jnp.bfloat16).reshape(-1, width)
    upward = jnp.dot(low_two, full_up, preferred_element_type=jnp.float32)
    active, gelu_back = jax.vjp(partial(jax.nn.gelu, approximate=False), upward)
    active_low = active.astype(jnp.bfloat16)
    layer_out = (
        attended
        + jnp.dot(active_low, full_down, preferred_element_type=jnp.float32).reshape(
            batch, rows, width
        )
    ).astype(jnp.bfloat16)
    grad_top = cotangent.astype(jnp.float32)
    grad_low = cotangent.reshape(-1, width)
    grad_down = dot_rows(active_low, grad_low)
    (grad_upward,) = gelu_back(dot_last(grad_low, full_down))
    upward_low = grad_upward.astype(jnp.bfloat16)
    grad_up = dot_rows(low_two, upward_low)
    grad_normed_two = dot_last(upward_low, full_up).reshape(batch, rows, width)
    back_mid, grad_ada_two_rows = back_two(grad_normed_two)
    grad_attended = grad_top + back_mid
    grad_ada_two = exact(cond.T, grad_ada_two_rows)
    attended_low = grad_attended.astype(jnp.bfloat16).reshape(-1, width)
    grad_out = dot_rows(mixed_flat, attended_low)
    grad_mixed = dot_last(attended_low, full_out).astype(jnp.bfloat16).reshape(batch, rows, width)

    def score_grads(
        query_item, keys_item, values_item, length, log_item, grad_item, query_place, key_spot
    ):
        scores = masked_scores(query_item, keys_item, length, query_place, key_spot)
        probs = jnp.exp(scores - log_item[..., None])
        grad_heads = split_heads(grad_item)
        grad_probs = jnp.einsum(
            "qhd,khd->hqk", grad_heads, split_heads(values_item), preferred_element_type=jnp.float32
        )
        inner = jnp.sum(probs * grad_probs, axis=-1, keepdims=True)
        grad_scores = (probs * (grad_probs - inner)).astype(jnp.bfloat16)
        return (probs, grad_heads, grad_scores, inner[..., 0])

    def attend_back(packed):
        query_item, keys_item, values_item, length, log_item, grad_item = packed
        probs, grad_heads, grad_scores, inner = score_grads(
            query_item, keys_item, values_item, length, log_item, grad_item, position, key_place
        )
        grad_query_item = (
            jnp.einsum(
                "hqk,khd->qhd",
                grad_scores,
                split_heads(keys_item),
                preferred_element_type=jnp.float32,
            )
            * scale
        )
        grad_keys_item = (
            jnp.einsum(
                "hqk,qhd->khd",
                grad_scores,
                split_heads(query_item),
                preferred_element_type=jnp.float32,
            )
            * scale
        )
        grad_values_item = jnp.einsum(
            "hqk,qhd->khd",
            probs.astype(jnp.bfloat16),
            grad_heads,
            preferred_element_type=jnp.float32,
        )
        return (
            grad_query_item.reshape(rows, width),
            grad_keys_item.reshape(frames_all, width),
            grad_values_item.reshape(frames_all, width),
        )

    grad_query_rows, grad_keys_all, grad_values_all = lax.map(
        attend_back, (query, keys_all, values_all, prompt_len, log_total, grad_mixed)
    )
    grad_keys_here, grad_values_here = (
        lax.psum_scatter(
            grad_keys_all.astype(jnp.bfloat16), "seq", scatter_dimension=1, tiled=True
        ).astype(jnp.float32),
        lax.psum_scatter(
            grad_values_all.astype(jnp.bfloat16), "seq", scatter_dimension=1, tiled=True
        ).astype(jnp.float32),
    )
    query_low = grad_query_rows.astype(jnp.bfloat16).reshape(-1, width)
    keys_low = grad_keys_here.astype(jnp.bfloat16).reshape(-1, width)
    values_low = grad_values_here.astype(jnp.bfloat16).reshape(-1, width)
    grad_query = dot_rows(low_one, query_low)
    grad_key = dot_rows(low_one, keys_low)
    grad_value = dot_rows(low_one, values_low)
    grad_normed_one = (
        dot_last(query_low, full_query)
        + dot_last(keys_low, full_key)
        + dot_last(values_low, full_value)
    )
    back_in, grad_ada_one_rows = back_one(grad_normed_one.reshape(batch, rows, width))
    input_grad = grad_attended + back_in
    grad_ada_one = exact(cond.T, grad_ada_one_rows)
    grad_cond = exact(grad_ada_one_rows, ada_one_w.T) + exact(grad_ada_two_rows, ada_two_w.T)
    grad_table = exact(choose.T, grad_cond)
    table_t = frames_major(grad_table, 1, items_count, seq_count)
    part_query = frames_major(grad_query, 0, items_count, seq_count)
    part_key = frames_major(grad_key, 0, items_count, seq_count)
    part_value = frames_major(grad_value, 0, items_count, seq_count)
    part_out = frames_major(grad_out, 0, items_count, seq_count)
    part_ada_one = frames_major(grad_ada_one, 0, items_count, seq_count)
    part_up = frames_major(grad_up, 0, items_count, seq_count)
    part_down = frames_major(grad_down, 0, items_count, seq_count)
    part_ada_two = frames_major(grad_ada_two, 0, items_count, seq_count)
    (
        seq_query,
        seq_key,
        seq_value,
        seq_out,
        seq_up,
        seq_down,
        seq_ada_one,
        seq_ada_two,
        seq_table,
    ) = (
        lax.psum_scatter(
            part_query.astype(jnp.bfloat16), "seq", scatter_dimension=0, tiled=True
        ).astype(jnp.float32),
        lax.psum_scatter(
            part_key.astype(jnp.bfloat16), "seq", scatter_dimension=0, tiled=True
        ).astype(jnp.float32),
        lax.psum_scatter(
            part_value.astype(jnp.bfloat16), "seq", scatter_dimension=0, tiled=True
        ).astype(jnp.float32),
        lax.psum_scatter(
            part_out.astype(jnp.bfloat16), "seq", scatter_dimension=0, tiled=True
        ).astype(jnp.float32),
        lax.psum_scatter(
            part_up.astype(jnp.bfloat16), "seq", scatter_dimension=0, tiled=True
        ).astype(jnp.float32),
        lax.psum_scatter(
            part_down.astype(jnp.bfloat16), "seq", scatter_dimension=0, tiled=True
        ).astype(jnp.float32),
        lax.psum_scatter(
            part_ada_one.astype(jnp.bfloat16), "seq", scatter_dimension=0, tiled=True
        ).astype(jnp.float32),
        lax.psum_scatter(
            part_ada_two.astype(jnp.bfloat16), "seq", scatter_dimension=0, tiled=True
        ).astype(jnp.float32),
        lax.psum_scatter(
            table_t.astype(jnp.bfloat16), "seq", scatter_dimension=1, tiled=True
        ).astype(jnp.float32),
    )
    (
        grad_query,
        grad_key,
        grad_value,
        grad_out,
        grad_up,
        grad_down,
        grad_ada_one,
        grad_ada_two,
        grad_table,
    ) = (
        lax.psum_scatter(
            seq_query.astype(jnp.bfloat16), "items", scatter_dimension=0, tiled=True
        ).astype(jnp.float32),
        lax.psum_scatter(
            seq_key.astype(jnp.bfloat16), "items", scatter_dimension=0, tiled=True
        ).astype(jnp.float32),
        lax.psum_scatter(
            seq_value.astype(jnp.bfloat16), "items", scatter_dimension=0, tiled=True
        ).astype(jnp.float32),
        lax.psum_scatter(
            seq_out.astype(jnp.bfloat16), "items", scatter_dimension=0, tiled=True
        ).astype(jnp.float32),
        lax.psum_scatter(
            seq_up.astype(jnp.bfloat16), "items", scatter_dimension=0, tiled=True
        ).astype(jnp.float32),
        lax.psum_scatter(
            seq_down.astype(jnp.bfloat16), "items", scatter_dimension=0, tiled=True
        ).astype(jnp.float32),
        lax.psum_scatter(
            seq_ada_one.astype(jnp.bfloat16), "items", scatter_dimension=0, tiled=True
        ).astype(jnp.float32),
        lax.psum_scatter(
            seq_ada_two.astype(jnp.bfloat16), "items", scatter_dimension=0, tiled=True
        ).astype(jnp.float32),
        lax.psum_scatter(
            seq_table.astype(jnp.bfloat16), "items", scatter_dimension=1, tiled=True
        ).astype(jnp.float32),
    )
    return (
        layer_out,
        input_grad,
        grad_query,
        grad_key,
        grad_value,
        grad_out,
        grad_up,
        grad_down,
        grad_ada_one,
        grad_ada_two,
        grad_table,
    )


def solution(mesh):
    return jax.shard_map(
        shards,
        mesh=mesh,
        in_specs=(
            P("items", "seq", None),
            P("items", "seq", None),
            P("items"),
            P("items"),
            P(),
            P("items", None),
            P("items", None),
            P("items", None),
            P("items", None),
            P("items", None),
            P("items", None),
            P("items", None),
            P("items", None),
        ),
        out_specs=(
            P("items", "seq", None),
            P("items", "seq", None),
            P(("items", "seq"), None),
            P(("items", "seq"), None),
            P(("items", "seq"), None),
            P(("items", "seq"), None),
            P(("items", "seq"), None),
            P(("items", "seq"), None),
            P(("items", "seq"), None),
            P(("items", "seq"), None),
            P(None, ("items", "seq")),
        ),
        check_vma=False,
    )
```

profile of v0, /device:TPU:0, one launch (start us, length us, event | category | flops | bytes accessed | tf_op | source)
XLA Modules:
  0.0 1794.8 jit_solution(3981334618277993144)
XLA Ops:
  14.1 49.4 %all-gather.13.cloned.1.call-done = bf16[1024,2048]{1,0:T(8,128)(2,1)} async-done(((bf16[64,2048]{1,0:T(8,128)(2,1)}), bf16[1024,2048]{1,0:T(8,128)(2,1)}) %all-gather.13.cloned.1.call-update) | async-done | bytes 4194320 | tf_op jit(solution)/shard_map/all_gather | solution.py:72
  63.5 3.9 fusion.75
  67.4 38.1 %all-gather.19.cloned.1.call-done = bf16[1024,1024]{1,0:T(8,128)(2,1)} async-done(((bf16[64,1024]{1,0:T(8,128)(2,1)}), bf16[1024,1024]{1,0:T(8,128)(2,1)}) %all-gather.19.cloned.1.call-update) | async-done | bytes 2097168 | tf_op jit(solution)/shard_map/all_gather | solution.py:67
  105.6 4.2 convolution_convert_fusion.1
  109.9 38.1 %all-gather.15.cloned.1.call-done = bf16[1024,1024]{1,0:T(8,128)(2,1)} async-done(((bf16[64,1024]{1,0:T(8,128)(2,1)}), bf16[1024,1024]{1,0:T(8,128)(2,1)}) %all-gather.15.cloned.1.call-update) | async-done | bytes 2097168 | tf_op jit(solution)/shard_map/all_gather | solution.py:68
  148.0 4.2 convolution_convert_fusion.3
  155.7 43.8 %all-gather.23.cloned.1.call-done = bf16[1024,2048]{1,0:T(8,128)(2,1)} async-done(((bf16[64,2048]{1,0:T(8,128)(2,1)}), bf16[1024,2048]{1,0:T(8,128)(2,1)}) %all-gather.23.cloned.1.call-update) | async-done | bytes 4194320 | tf_op jit(solution)/shard_map/all_gather | solution.py:73
  199.5 3.9 fusion.73
  203.4 38.0 %all-gather.17.cloned.1.call-done = bf16[1024,1024]{1,0:T(8,128)(2,1)} async-done(((bf16[64,1024]{1,0:T(8,128)(2,1)}), bf16[1024,1024]{1,0:T(8,128)(2,1)}) %all-gather.17.cloned.1.call-update) | async-done | bytes 2097168 | tf_op jit(solution)/shard_map/all_gather | solution.py:66
  241.5 3.2 convolution_convert_fusion.2
  246.1 35.2 %all-gather.31.cloned.1.call-done = bf16[1280,1024]{1,0:T(8,128)(2,1)} async-done(((bf16[640,1024]{1,0:T(8,128)(2,1)}), bf16[1280,1024]{1,0:T(8,128)(2,1)}) %all-gather.31.cloned.1.call-update) | async-done | bytes 2621456 | tf_op jit(solution)/shard_map/all_gather | solution.py:109
  281.3 3.0 copy.60
  284.3 23.1 %fusion.93 = (f32[16,640]{1,0:T(8,128)S(1)}, f32[16,640,1280]{2,1,0:T(8,128)}) fusion(bf16[640,16,64]{0,2,1:T(8,128)(2,1)} %bitcast.284, bf16[1280,16,64]{0,2,1:T(8,128)(2,1)S(1)} %bitcast.278, pred[640,1280]{1,0:T(8,128)(4,1)S(1)} %and_or_fusion), kind=kOutput, calls=%fused_computation.153 | convolution fusion | flops 1717032960 | bytes 57221120 | tf_op jit(solution)/shard_map/while/body/eval_jaxpr/qhd,khd->hqk/dot_general | solution.py:115
  307.4 16.8 fusion
  324.2 4.4 copy.58
  328.6 20.2 %fusion.50 = bf16[16,64,640]{2,1,0:T(8,128)(2,1)S(1)} fusion(bf16[1280,16,64]{0,2,1:T(8,128)(2,1)} %bitcast.289, f32[16,640,1280]{2,1,0:T(8,128)} %get-tuple-element.90, f32[16,640]{1,0:T(8,128)S(1)} %fusion, f32[16,640]{1,0:T(8,128)S(1)} %get-tuple-element.89), kind=kOutput, calls=%fused_computation.97 | convolution fusion | flops 1717698560 | bytes 56442880 | tf_op jit(solution)/shard_map/while/body/eval_jaxpr/hqk,khd->qhd/dot_general | solution.py:135
  348.8 17.3 all-gather.21.cloned.1.call-done
  366.1 3.2 fusion.94
  371.3 70.7 %all-gather.25.cloned.1.call-done = bf16[1024,4096]{1,0:T(8,128)(2,1)} async-done(((bf16[64,4096]{1,0:T(8,128)(2,1)}), bf16[1024,4096]{1,0:T(8,128)(2,1)}) %all-gather.25.cloned.1.call-update) | async-done | bytes 8388624 | tf_op jit(solution)/shard_map/all_gather | solution.py:70
  442.0 32.4 %fusion.6 = (f32[640,4096]{1,0:T(8,128)}, f32[640,4096]{1,0:T(8,128)}) fusion(bf16[1024,4096]{1,0:T(8,128)(2,1)} %all-gather.25.cloned.1.call-done, f32[1024]{0:T(1024)S(1)} %bitcast.330, f32[640]{0:T(1024)S(1)} %fusion.78, f32[1,640,1024]{2,1,0:T(8,128)} %copy-done.6, f32[640]{0:T(1024)S(1)} %broadcast_multiply_fusion, f32[1024]{0:T(1024)S(1)} %bitcast.310), kind=kOutput, calls=%fused_computation.13 | convolution fusion | flops 5534515200 | bytes 31994880 | tf_op jit(solution)/shard_map/dot_general | solution.py:150
  474.4 42.8 %all-gather.27.cloned.1.call-done = bf16[4096,1024]{1,0:T(8,128)(2,1)} async-done(((bf16[256,1024]{1,0:T(8,128)(2,1)}), bf16[4096,1024]{1,0:T(8,128)(2,1)}) %all-gather.27.cloned.1.call-update) | async-done | bytes 8388624 | tf_op jit(solution)/shard_map/all_gather | solution.py:71
  517.2 16.8 add_convert_fusion
  533.9 10.2 fusion.95
  544.2 2.1 fusion.46
  552.4 38.6 %multiply_reduce_fusion = (f32[16,640]{1,0:T(8,128)S(1)}, f32[16,640,1280]{2,1,0:T(8,128)}) fusion(f32[16,640,1280]{2,1,0:T(8,128)} %get-tuple-element.90, f32[16,640]{1,0:T(8,128)S(1)} %log_add_fusion, bf16[640,16,64]{0,2,1:T(8,128)(2,1)S(1)} %bitcast.287, bf16[1280,16,64]{0,2,1:T(8,128)(2,1)} %bitcast.290), kind=kOutput, calls=%fused_computation.1 | convolution fusion | flops 1717032960 | bytes 108871680 | tf_op jit(solution)/shard_map/while/body/eval_jaxpr/qhd,khd->hqk/dot_general | solution.py:179
  591.0 42.2 %multiply_convert_fusion = bf16[16,640,1280]{2,1,0:T(8,128)(2,1)} fusion(f32[16,640,1280]{2,1,0:T(8,128)} %get-tuple-element.96, f32[16,640,1280]{2,1,0:T(8,128)} %get-tuple-element.90, f32[16,640]{1,0:T(8,128)S(1)} %get-tuple-element.95, f32[16,640]{1,0:T(8,128)S(1)} %log_add_fusion), kind=kLoop, calls=%fused_computation | loop fusion | flops 52428800 | bytes 131153920 | tf_op jit(solution)/shard_map/while/body/eval_jaxpr/convert_element_type | solution.py:183
  633.2 14.6 multiply_convert_fusion.5
  647.8 4.5 copy.62
  652.4 21.5 %fusion.36 = bf16[16,64,1280]{2,1,0:T(8,128)(2,1)} fusion(bf16[640,16,64]{0,2,1:T(8,128)(2,1)S(1)} %bitcast.288, f32[16,640,1280]{2,1,0:T(8,128)} %get-tuple-element.90, f32[16,640]{1,0:T(8,128)S(1)} %log_add_fusion), kind=kOutput, calls=%fused_computation.67 | convolution fusion | flops 1705246720 | bytes 56401920 | tf_op jit(solution)/shard_map/while/body/eval_jaxpr/hqk,qhd->khd/dot_general | solution.py:209
  673.9 4.5 copy.63
  678.5 5.7 fusion.69
  684.2 14.9 multiply_convert_fusion.6
  699.0 5.2 fusion.96
  704.2 4.4 fusion.56
  708.7 19.5 %reduce-scatter.25.cloned.1.call-done = bf16[1,640,1024]{2,1,0:T(8,128)(2,1)} async-done(((bf16[1,1280,1024]{2,1,0:T(8,128)(2,1)}), bf16[1,640,1024]{2,1,0:T(8,128)(2,1)}) %reduce-scatter.25.cloned.1.call-update) | async-done | bytes 1310736 | tf_op jit(solution)/shard_map/reduce_scatter | solution.py:228
  728.2 5.9 fusion.45
  734.7 2.5 fusion.43
  737.2 5.5 fusion.71
  744.1 3.5 convert_bitcast_fusion.2
  749.3 4.5 fusion.90
  759.3 1.8 convert_bitcast_fusion.5
  766.8 6.4 multiply_convert_fusion.2
  775.4 11.5 convert_bitcast_fusion.1
  786.9 7.8 copy.71
  794.7 24.6 %fusion.9 = bf16[4096,640]{0,1:T(8,128)(2,1)} fusion(f32[640,4096]{1,0:T(8,128)} %get-tuple-element.94), kind=kLoop, calls=%fused_computation.16 | loop fusion | flops 170393600 | bytes 15728640 | tf_op jit(solution)/shard_map/convert_element_type | solution.py:152
  819.4 7.9 copy.83
  827.3 11.6 convert_bitcast_fusion
  838.9 8.2 copy.73
  850.1 5.5 reduce-scatter.27.cloned.1.call-done
  855.6 34.0 %reduce-scatter.31.cloned.1.call-done = bf16[512,1024]{1,0:T(8,128)(2,1)} async-done(((bf16[1024,1024]{1,0:T(8,128)(2,1)}), bf16[512,1024]{1,0:T(8,128)(2,1)}) %reduce-scatter.31.cloned.1.call-update) | async-done | bytes 1048592 | tf_op jit(solution)/shard_map/reduce_scatter | solution.py:271
  889.7 56.4 %reduce-scatter.55.cloned.1.call-done = bf16[512,2048]{1,0:T(8,128)(2,1)} async-done(((bf16[1024,2048]{1,0:T(8,128)(2,1)}), bf16[512,2048]{1,0:T(8,128)(2,1)}) %reduce-scatter.55.cloned.1.call-update) | async-done | bytes 2097168 | tf_op jit(solution)/shard_map/reduce_scatter | solution.py:289
  946.2 56.7 %reduce-scatter.51.cloned.1.call-done = bf16[512,2048]{1,0:T(8,128)(2,1)} async-done(((bf16[1024,2048]{1,0:T(8,128)(2,1)}), bf16[512,2048]{1,0:T(8,128)(2,1)}) %reduce-scatter.51.cloned.1.call-update) | async-done | bytes 2097168 | tf_op jit(solution)/shard_map/reduce_scatter | solution.py:286
  1002.9 101.3 %reduce-scatter.43.cloned.1.call-done = bf16[512,4096]{1,0:T(8,128)(2,1)} async-done(((bf16[1024,4096]{1,0:T(8,128)(2,1)}), bf16[512,4096]{1,0:T(8,128)(2,1)}) %reduce-scatter.43.cloned.1.call-update) | async-done | bytes 4194320 | tf_op jit(solution)/shard_map/reduce_scatter | solution.py:280
  1104.5 101.4 %reduce-scatter.47.cloned.1.call-done = bf16[2048,1024]{1,0:T(8,128)(2,1)} async-done(((bf16[4096,1024]{1,0:T(8,128)(2,1)}), bf16[2048,1024]{1,0:T(8,128)(2,1)}) %reduce-scatter.47.cloned.1.call-update) | async-done | bytes 4194320 | tf_op jit(solution)/shard_map/reduce_scatter | solution.py:283
  1206.0 13.2 fusion.48
  1219.1 45.9 %reduce-scatter.61.cloned.1.call-done = bf16[32,8]{1,0:T(8,128)(2,1)} async-done(((bf16[512,8]{1,0:T(8,128)(2,1)}), bf16[32,8]{1,0:T(8,128)(2,1)}) %reduce-scatter.61.cloned.1.call-update) | async-done | bytes 528
  1266.4 58.7 %reduce-scatter.41.cloned.1.call-done = bf16[32,1024]{1,0:T(8,128)(2,1)} async-done(((bf16[512,1024]{1,0:T(8,128)(2,1)}), bf16[32,1024]{1,0:T(8,128)(2,1)}) %reduce-scatter.41.cloned.1.call-update) | async-done | bytes 65552 | tf_op jit(solution)/shard_map/reduce_scatter | solution.py:316
  1326.6 58.9 %reduce-scatter.37.cloned.1.call-done = bf16[32,1024]{1,0:T(8,128)(2,1)} async-done(((bf16[512,1024]{1,0:T(8,128)(2,1)}), bf16[32,1024]{1,0:T(8,128)(2,1)}) %reduce-scatter.37.cloned.1.call-update) | async-done | bytes 65552 | tf_op jit(solution)/shard_map/reduce_scatter | solution.py:313
  1387.1 58.5 %reduce-scatter.29.cloned.1.call-done = bf16[32,1024]{1,0:T(8,128)(2,1)} async-done(((bf16[512,1024]{1,0:T(8,128)(2,1)}), bf16[32,1024]{1,0:T(8,128)(2,1)}) %reduce-scatter.29.cloned.1.call-update) | async-done | bytes 65552 | tf_op jit(solution)/shard_map/reduce_scatter | solution.py:307
  1447.0 58.9 %reduce-scatter.33.cloned.1.call-done = bf16[32,1024]{1,0:T(8,128)(2,1)} async-done(((bf16[512,1024]{1,0:T(8,128)(2,1)}), bf16[32,1024]{1,0:T(8,128)(2,1)}) %reduce-scatter.33.cloned.1.call-update) | async-done | bytes 65552 | tf_op jit(solution)/shard_map/reduce_scatter | solution.py:310
  1507.4 62.7 %reduce-scatter.57.cloned.1.call-done = bf16[32,2048]{1,0:T(8,128)(2,1)} async-done(((bf16[512,2048]{1,0:T(8,128)(2,1)}), bf16[32,2048]{1,0:T(8,128)(2,1)}) %reduce-scatter.57.cloned.1.call-update) | async-done | bytes 131088 | tf_op jit(solution)/shard_map/reduce_scatter | solution.py:328
  1571.8 63.1 %reduce-scatter.53.cloned.1.call-done = bf16[32,2048]{1,0:T(8,128)(2,1)} async-done(((bf16[512,2048]{1,0:T(8,128)(2,1)}), bf16[32,2048]{1,0:T(8,128)(2,1)}) %reduce-scatter.53.cloned.1.call-update) | async-done | bytes 131088 | tf_op jit(solution)/shard_map/reduce_scatter | solution.py:325
  1636.5 73.8 %reduce-scatter.45.cloned.1.call-done = bf16[32,4096]{1,0:T(8,128)(2,1)} async-done(((bf16[512,4096]{1,0:T(8,128)(2,1)}), bf16[32,4096]{1,0:T(8,128)(2,1)}) %reduce-scatter.45.cloned.1.call-update) | async-done | bytes 262160 | tf_op jit(solution)/shard_map/reduce_scatter | solution.py:319
  1712.1 73.8 %reduce-scatter.49.cloned.1.call-done = bf16[128,1024]{1,0:T(8,128)(2,1)} async-done(((bf16[2048,1024]{1,0:T(8,128)(2,1)}), bf16[128,1024]{1,0:T(8,128)(2,1)}) %reduce-scatter.49.cloned.1.call-update) | async-done | bytes 262160 | tf_op jit(solution)/shard_map/reduce_scatter | solution.py:322
  (184 shorter events, 52.9 us)
Async XLA Ops:
  7.2 6.8 copy-start
  7.2 5.7 copy-start.4
  7.2 56.3 %all-gather.13.cloned.1.call-start = ((), (), s32[]{:S(2)}) async-start(), calls=%async_computation.20 | async-start | bytes 4456448 | tf_op jit(solution)/shard_map/all_gather | solution.py:72
  7.9 97.6 %all-gather.19.cloned.1.call-start = ((), (), s32[]{:S(2)}) async-start(), calls=%async_computation.23 | async-start | bytes 2228224 | tf_op jit(solution)/shard_map/all_gather | solution.py:67
  8.7 139.3 %all-gather.15.cloned.1.call-start = ((), (), s32[]{:S(2)}) async-start(), calls=%async_computation.21 | async-start | bytes 2228224 | tf_op jit(solution)/shard_map/all_gather | solution.py:68
  9.4 190.1 %all-gather.23.cloned.1.call-start = ((), (), s32[]{:S(2)}) async-start(), calls=%async_computation.25 | async-start | bytes 4456448 | tf_op jit(solution)/shard_map/all_gather | solution.py:73
  10.0 231.5 %all-gather.17.cloned.1.call-start = ((), (), s32[]{:S(2)}) async-start(), calls=%async_computation.22 | async-start | bytes 2228224 | tf_op jit(solution)/shard_map/all_gather | solution.py:66
  10.6 270.7 %all-gather.31.cloned.1.call-start = ((), (), s32[]{:S(2)}) async-start(), calls=%async_computation.48 | async-start | bytes 3932160 | tf_op jit(solution)/shard_map/all_gather | solution.py:109
  12.9 228.6 %copy-start.17 = (f32[640]{0:T(1024)}, f32[640]{0:T(1024)S(1)}, u32[]{:S(2)}) copy-start(f32[640]{0:T(1024)S(1)} %broadcast_multiply_fusion.1) | copy-start | bytes 7684
  13.3 0.6 copy-start.25
  13.9 227.5 %copy-start.21 = (f32[640]{0:T(1024)}, f32[640]{0:T(1024)S(1)}, u32[]{:S(2)}) copy-start(f32[640]{0:T(1024)S(1)} %fusion.77) | copy-start | bytes 7684
  14.1 185.4 %copy-start.23 = (f32[1,1024]{1,0:T(1,128)}, f32[1,1024]{1,0:T(1,128)S(1)}, u32[]{:S(2)}) copy-start(f32[1,1024]{1,0:T(1,128)S(1)} %fusion.79) | copy-start | bytes 12292
  67.4 174.1 %copy-start.19 = (f32[1,1024]{1,0:T(1,128)}, f32[1,1024]{1,0:T(1,128)S(1)}, u32[]{:S(2)}) copy-start(f32[1,1024]{1,0:T(1,128)S(1)} %get-tuple-element.87) | copy-start | bytes 12292
  67.4 174.0 %copy-start.27 = (f32[1,1024]{1,0:T(1,128)}, f32[1,1024]{1,0:T(1,128)S(1)}, u32[]{:S(2)}) copy-start(f32[1,1024]{1,0:T(1,128)S(1)} %get-tuple-element.88) | copy-start | bytes 12292
  109.8 214.4 %all-gather.29.cloned.1.call-start = ((), (), s32[]{:S(2)}) async-start(), calls=%async_computation.47 | async-start | bytes 3932160 | tf_op jit(solution)/shard_map/all_gather | solution.py:110
  152.2 213.9 %all-gather.21.cloned.1.call-start = ((), (), s32[]{:S(2)}) async-start(), calls=%async_computation.24 | async-start | bytes 2228224 | tf_op jit(solution)/shard_map/all_gather | solution.py:69
  153.0 289.0 %all-gather.25.cloned.1.call-start = ((), (), s32[]{:S(2)}) async-start(), calls=%async_computation.26 | async-start | bytes 8912896 | tf_op jit(solution)/shard_map/all_gather | solution.py:70
  153.7 363.5 %all-gather.27.cloned.1.call-start = ((), (), s32[]{:S(2)}) async-start(), calls=%async_computation.27 | async-start | bytes 8912896 | tf_op jit(solution)/shard_map/all_gather | solution.py:71
  154.3 550.0 %reduce-scatter.23.cloned.1.call-start = ((), (), s32[]{:S(2)}) async-start(), calls=%async_computation.28 | async-start | bytes 3932160 | tf_op jit(solution)/shard_map/reduce_scatter | solution.py:225
  284.2 23.1 %copy-start.2 = (bf16[1280,1024]{0,1:T(8,128)(2,1)}, bf16[1280,1024]{0,1:T(8,128)(2,1)S(1)}, u32[]{:S(2)}) copy-start(bf16[1280,1024]{0,1:T(8,128)(2,1)S(1)} %copy.60) | copy-start | bytes 7864324
  328.6 37.5 %copy-start.5 = (bf16[1,640,1024]{2,1,0:T(8,128)(2,1)S(1)}, bf16[1,640,1024]{2,1,0:T(8,128)(2,1)}, u32[]{:S(2)}) copy-start(bf16[1,640,1024]{2,1,0:T(8,128)(2,1)} %param.13) | copy-start | bytes 3932164
  348.8 20.6 %copy-start.32 = (bf16[16,64,640]{2,1,0:T(8,128)(2,1)}, bf16[16,64,640]{2,1,0:T(8,128)(2,1)S(1)}, u32[]{:S(2)}) copy-start(bf16[16,64,640]{2,1,0:T(8,128)(2,1)S(1)} %fusion.50) | copy-start | bytes 3932164
  369.3 1.5 copy-start.6
  442.0 75.2 %copy-start.12 = (bf16[1,640,1024]{2,1,0:T(8,128)(2,1)S(1)}, bf16[1,640,1024]{2,1,0:T(8,128)(2,1)}, u32[]{:S(2)}) copy-start(bf16[1,640,1024]{2,1,0:T(8,128)(2,1)} %param.14) | copy-start | bytes 3932164
  533.9 10.3 copy-start.7
  547.2 1.5 copy-start.9
  547.2 2.8 copy-start.30
  548.6 1.0 copy-start.16
  591.0 42.2 %copy-start.10 = (bf16[640,1024]{0,1:T(8,128)(2,1)S(1)}, bf16[640,1024]{0,1:T(8,128)(2,1)}, u32[]{:S(2)}) copy-start(bf16[640,1024]{0,1:T(8,128)(2,1)} %copy.59) | copy-start | bytes 3932164
  652.4 75.8 %reduce-scatter.25.cloned.1.call-start = ((), (), s32[]{:S(2)}) async-start(), calls=%async_computation.29 | async-start | bytes 3932160 | tf_op jit(solution)/shard_map/reduce_scatter | solution.py:228
  678.4 5.8 copy-start.3
  678.4 168.8 %reduce-scatter.59.cloned.1.call-start = ((), (), s32[]{:S(2)}) async-start(), calls=%async_computation.46 | async-start | bytes 24576 | tf_op jit(solution)/shard_map/reduce_scatter | solution.py:292
  699.0 5.2 copy-start.29
  704.2 23.9 %copy-start.18 = (f32[640]{0:T(1024)S(1)}, f32[640]{0:T(1024)}, u32[]{:S(2)}) copy-start(f32[640]{0:T(1024)} %copy-done.17) | copy-start | bytes 7684
  704.2 23.9 %copy-start.20 = (f32[1,1024]{1,0:T(1,128)S(1)}, f32[1,1024]{1,0:T(1,128)}, u32[]{:S(2)}) copy-start(f32[1,1024]{1,0:T(1,128)} %copy-done.19) | copy-start | bytes 12292
  708.7 25.4 %copy-start.26 = (f32[640]{0:T(1024)S(1)}, f32[640]{0:T(1024)}, u32[]{:S(2)}) copy-start(f32[640]{0:T(1024)} %copy-done.25) | copy-start | bytes 7684
  734.0 0.7 copy-start.22
  743.7 105.1 %reduce-scatter.39.cloned.1.call-start = ((), (), s32[]{:S(2)}) async-start(), calls=%async_computation.36 | async-start | bytes 3145728 | tf_op jit(solution)/shard_map/reduce_scatter | solution.py:277
  747.6 1.6 copy-start.28
  749.2 100.3 %reduce-scatter.35.cloned.1.call-start = ((), (), s32[]{:S(2)}) async-start(), calls=%async_computation.34 | async-start | bytes 3145728 | tf_op jit(solution)/shard_map/reduce_scatter | solution.py:274
  753.8 1.8 copy-start.15
  757.4 1.8 copy-start.14
  758.9 96.6 %reduce-scatter.27.cloned.1.call-start = ((), (), s32[]{:S(2)}) async-start(), calls=%async_computation.30 | async-start | bytes 3145728 | tf_op jit(solution)/shard_map/reduce_scatter | solution.py:268
  761.1 2.2 copy-start.31
  762.6 127.0 %reduce-scatter.31.cloned.1.call-start = ((), (), s32[]{:S(2)}) async-start(), calls=%async_computation.32 | async-start | bytes 3145728 | tf_op jit(solution)/shard_map/reduce_scatter | solution.py:271
  765.1 1.6 copy-start.24
  766.7 179.4 %reduce-scatter.55.cloned.1.call-start = ((), (), s32[]{:S(2)}) async-start(), calls=%async_computation.44 | async-start | bytes 6291456 | tf_op jit(solution)/shard_map/reduce_scatter | solution.py:289
  773.3 1.3 copy-start.11
  773.3 229.5 %reduce-scatter.51.cloned.1.call-start = ((), (), s32[]{:S(2)}) async-start(), calls=%async_computation.42 | async-start | bytes 6291456 | tf_op jit(solution)/shard_map/reduce_scatter | solution.py:286
  774.1 330.2 %reduce-scatter.43.cloned.1.call-start = ((), (), s32[]{:S(2)}) async-start(), calls=%async_computation.38 | async-start | bytes 12582912 | tf_op jit(solution)/shard_map/reduce_scatter | solution.py:280
  794.7 411.2 %reduce-scatter.47.cloned.1.call-start = ((), (), s32[]{:S(2)}) async-start(), calls=%async_computation.40 | async-start | bytes 12582912 | tf_op jit(solution)/shard_map/reduce_scatter | solution.py:283
  819.4 7.9 copy-start.13
  847.1 417.9 %reduce-scatter.61.cloned.1.call-start = ((), (), s32[]{:S(2)}) async-start(), calls=%async_computation.49 | async-start | bytes 139264
  848.7 476.4 %reduce-scatter.41.cloned.1.call-start = ((), (), s32[]{:S(2)}) async-start(), calls=%async_computation.37 | async-start | bytes 1114112 | tf_op jit(solution)/shard_map/reduce_scatter | solution.py:316
  849.5 536.1 %reduce-scatter.37.cloned.1.call-start = ((), (), s32[]{:S(2)}) async-start(), calls=%async_computation.35 | async-start | bytes 1114112 | tf_op jit(solution)/shard_map/reduce_scatter | solution.py:313
  850.0 595.5 %reduce-scatter.29.cloned.1.call-start = ((), (), s32[]{:S(2)}) async-start(), calls=%async_computation.31 | async-start | bytes 1114112 | tf_op jit(solution)/shard_map/reduce_scatter | solution.py:307
  855.6 650.3 %reduce-scatter.33.cloned.1.call-start = ((), (), s32[]{:S(2)}) async-start(), calls=%async_computation.33 | async-start | bytes 1114112 | tf_op jit(solution)/shard_map/reduce_scatter | solution.py:310
  889.6 680.5 %reduce-scatter.57.cloned.1.call-start = ((), (), s32[]{:S(2)}) async-start(), calls=%async_computation.45 | async-start | bytes 2228224 | tf_op jit(solution)/shard_map/reduce_scatter | solution.py:328
  946.1 688.8 %reduce-scatter.53.cloned.1.call-start = ((), (), s32[]{:S(2)}) async-start(), calls=%async_computation.43 | async-start | bytes 2228224 | tf_op jit(solution)/shard_map/reduce_scatter | solution.py:325
  1002.9 707.5 %reduce-scatter.45.cloned.1.call-start = ((), (), s32[]{:S(2)}) async-start(), calls=%async_computation.39 | async-start | bytes 4456448 | tf_op jit(solution)/shard_map/reduce_scatter | solution.py:319
  1104.3 101.7 %copy-start.8 = (f32[1,640,1024]{2,1,0:T(8,128)S(1)}, f32[1,640,1024]{2,1,0:T(8,128)}, u32[]{:S(2)}) copy-start(f32[1,640,1024]{2,1,0:T(8,128)} %copy-done.6) | copy-start | bytes 7864324
  1104.3 681.6 %reduce-scatter.49.cloned.1.call-start = ((), (), s32[]{:S(2)}) async-start(), calls=%async_computation.41 | async-start | bytes 4456448 | tf_op jit(solution)/shard_map/reduce_scatter | solution.py:322
  1206.0 581.7 %copy-start.1 = (bf16[8,1024]{1,0:T(8,128)(2,1)S(1)}, bf16[8,1024]{1,0:T(8,128)(2,1)}, u32[]{:S(2)}) copy-start(bf16[8,1024]{1,0:T(8,128)(2,1)} %param.17) | copy-start | bytes 49156
Sparse Core Ops, SparseCore 0:
  10.2 53.2 all-gather.12
  65.7 39.8 all-gather.18
  107.7 40.1 all-gather.14
  150.0 49.4 all-gather.22
  201.5 39.9 all-gather.16
  243.4 37.7 all-gather.30
  283.4 39.0 all-gather.28
  324.6 41.4 all-gather.20
  368.3 73.6 all-gather.24
  444.0 73.1 all-gather.26
  652.5 35.8 reduce-scatter.22
  690.5 37.5 reduce-scatter.24
  743.8 9.7 reduce-scatter.58
  755.7 31.8 reduce-scatter.38
  789.7 31.8 reduce-scatter.34
  823.7 31.8 reduce-scatter.26
  857.7 31.8 reduce-scatter.30
  891.8 54.2 reduce-scatter.54
  948.5 54.3 reduce-scatter.50
  1005.0 99.2 reduce-scatter.42
  1106.7 99.2 reduce-scatter.46
  1210.0 55.0 reduce-scatter.60
  1268.7 56.3 reduce-scatter.40
  1329.0 56.4 reduce-scatter.36
  1389.2 56.3 reduce-scatter.28
  1449.5 56.4 reduce-scatter.32
  1509.5 60.5 reduce-scatter.56
  1574.3 60.5 reduce-scatter.52
  1638.8 71.5 reduce-scatter.44
  1714.5 71.3 reduce-scatter.48
where the time goes:
time: 1800 us; the launch traced here: 1790 us
  waiting for transfers between devices  1310 us (73%)
  matrix products  288 us (16%)
  other arithmetic  117 us (6%)
  local copies, waits for them, and re-layouts  60.6 us (3%)
    reduce_scatter x1, waiting for transfers between devices, shards(): lax.psum_scatter(part_down.astype(jnp.bfloat16), 'seq', scatter_dimension...  101 us
    reduce_scatter x1, waiting for transfers between devices, shards(): lax.psum_scatter(part_up.astype(jnp.bfloat16), 'seq', scatter_dimension=0...  101 us
    reduce_scatter x1, waiting for transfers between devices, shards(): lax.psum_scatter(seq_up.astype(jnp.bfloat16), 'items', scatter_dimension=...  73.8 us
    reduce_scatter x1, waiting for transfers between devices, shards(): lax.psum_scatter(seq_down.astype(jnp.bfloat16), 'items', scatter_dimensio...  73.8 us
    all_gather x1, waiting for transfers between devices, shards(): lax.all_gather(w_up, 'items', axis=0, tiled=True)  70.7 us
    reduce_scatter x1, waiting for transfers between devices, shards(): lax.psum_scatter(seq_ada_one.astype(jnp.bfloat16), 'items', scatter_dimen...  63.1 us
    reduce_scatter x1, waiting for transfers between devices, shards(): lax.psum_scatter(seq_ada_two.astype(jnp.bfloat16), 'items', scatter_dimen...  62.7 us
    reduce_scatter x1, waiting for transfers between devices, shards(): lax.psum_scatter(seq_value.astype(jnp.bfloat16), 'items', scatter_dimensi...  58.9 us
  transfers between devices with their start and end apart: 30, of which 25 were waited for; matrix products, arithmetic and copies ran while one was open for 17% of the time, Pallas kernels for 0%

commit v1 on v0

--- a/solution.py
+++ b/solution.py
@@ -67,7 +67,9 @@
         lax.all_gather(w_key, "items", axis=0, tiled=True),
         lax.all_gather(w_value, "items", axis=0, tiled=True),
         lax.all_gather(w_out, "items", axis=0, tiled=True),
-        lax.all_gather(w_up, "items", axis=0, tiled=True),
+        jnp.concatenate(
+            lax.all_to_all(jnp.stack([w_up] * lax.axis_size("items")), "items", 0, 0), axis=0
+        ),
         lax.all_gather(w_down, "items", axis=0, tiled=True),
         lax.all_gather(w_ada_one, "items", axis=0, tiled=True),
         lax.all_gather(w_ada_two, "items", axis=0, tiled=True),

time: 1800 us -> 1840 us (1.022)
  waiting for transfers between devices: 1310 us -> 1350 us
    all_gather x1, waiting for transfers between devices: 38 us -> 127 us  [shards(): lax.all_gather(w_query, 'items', axis=0, tiled=True)]
    all_gather x1 -> x0, waiting for transfers between devices: 70.7 us -> none  [shards(): lax.all_gather(w_up, 'items', axis=0, tiled=True)]
    all_gather x1, waiting for transfers between devices: 0.02 us -> 38.2 us  [shards(): lax.all_gather(values_here, 'seq', axis=1, tiled=True)]
    all_gather x1, waiting for transfers between devices: 42.8 us -> 18.4 us  [shards(): lax.all_gather(w_down, 'items', axis=0, tiled=True)]
    all_gather x1, waiting for transfers between devices: 43.8 us -> 64.1 us  [shards(): lax.all_gather(w_ada_two, 'items', axis=0, tiled=True)]
    unnamed x31 -> x30, waiting for transfers between devices: 53.1 us -> 52.6 us
  transfers between devices with their start and end apart: 30 -> 30, of which waited for: 25 -> 24; matrix products, arithmetic and copies ran while one was open for 17% -> 17% of each run, Pallas kernels for 0% -> 0%
where the time goes in v1:
time: 1840 us
  waiting for transfers between devices  1350 us (73%)
  matrix products  286 us (16%)
  other arithmetic  118 us (6%)
  local copies, waits for them, and re-layouts  64.6 us (4%)
    all_gather x1, waiting for transfers between devices, shards(): lax.all_gather(w_query, 'items', axis=0, tiled=True)  127 us
    reduce_scatter x1, waiting for transfers between devices, shards(): lax.psum_scatter(part_up.astype(jnp.bfloat16), 'seq', scatter_dimension=0...  101 us
    reduce_scatter x1, waiting for transfers between devices, shards(): lax.psum_scatter(part_down.astype(jnp.bfloat16), 'seq', scatter_dimension...  101 us
    reduce_scatter x1, waiting for transfers between devices, shards(): lax.psum_scatter(seq_down.astype(jnp.bfloat16), 'items', scatter_dimensio...  74.1 us
    reduce_scatter x1, waiting for transfers between devices, shards(): lax.psum_scatter(seq_up.astype(jnp.bfloat16), 'items', scatter_dimension=...  73.8 us
    all_gather x1, waiting for transfers between devices, shards(): lax.all_gather(w_ada_two, 'items', axis=0, tiled=True)  64.1 us
    reduce_scatter x1, waiting for transfers between devices, shards(): lax.psum_scatter(seq_ada_one.astype(jnp.bfloat16), 'items', scatter_dimen...  63 us
    reduce_scatter x1, waiting for transfers between devices, shards(): lax.psum_scatter(seq_ada_two.astype(jnp.bfloat16), 'items', scatter_dimen...  62.7 us
  transfers between devices with their start and end apart: 30, of which 24 were waited for; matrix products, arithmetic and copies ran while one was open for 17% of the time, Pallas kernels for 0%

profile of v1, /device:TPU:0, one launch (start us, length us, event | category | flops | bytes accessed | tf_op | source)
XLA Modules:
  0.0 1838.2 jit_solution(10187829405015419222)
XLA Ops:
  13.5 50.0 %all-gather.12.cloned.1.call-done = bf16[1024,2048]{1,0:T(8,128)(2,1)} async-done(((bf16[64,2048]{1,0:T(8,128)(2,1)}), bf16[1024,2048]{1,0:T(8,128)(2,1)}) %all-gather.12.cloned.1.call-update) | async-done | bytes 4194320 | tf_op jit(solution)/shard_map/all_gather | solution.py:74
  63.5 3.9 fusion.75
  67.4 38.1 %all-gather.18.cloned.1.call-done = bf16[1024,1024]{1,0:T(8,128)(2,1)} async-done(((bf16[64,1024]{1,0:T(8,128)(2,1)}), bf16[1024,1024]{1,0:T(8,128)(2,1)}) %all-gather.18.cloned.1.call-update) | async-done | bytes 2097168 | tf_op jit(solution)/shard_map/all_gather | solution.py:67
  105.6 4.2 convolution_convert_fusion.1
  109.9 38.1 %all-gather.14.cloned.1.call-done = bf16[1024,1024]{1,0:T(8,128)(2,1)} async-done(((bf16[64,1024]{1,0:T(8,128)(2,1)}), bf16[1024,1024]{1,0:T(8,128)(2,1)}) %all-gather.14.cloned.1.call-update) | async-done | bytes 2097168 | tf_op jit(solution)/shard_map/all_gather | solution.py:68
  148.0 4.2 convolution_convert_fusion.3
  153.0 4.3 stack.2
  157.3 4.7 all-to-all-start
  164.2 126.6 %all-gather.16.cloned.1.call-done = bf16[1024,1024]{1,0:T(8,128)(2,1)} async-done(((bf16[64,1024]{1,0:T(8,128)(2,1)}), bf16[1024,1024]{1,0:T(8,128)(2,1)}) %all-gather.16.cloned.1.call-update) | async-done | bytes 2097168 | tf_op jit(solution)/shard_map/all_gather | solution.py:66
  290.8 3.2 convolution_convert_fusion.2
  295.4 64.1 %all-gather.22.cloned.1.call-done = bf16[1024,2048]{1,0:T(8,128)(2,1)} async-done(((bf16[64,2048]{1,0:T(8,128)(2,1)}), bf16[1024,2048]{1,0:T(8,128)(2,1)}) %all-gather.22.cloned.1.call-update) | async-done | bytes 4194320 | tf_op jit(solution)/shard_map/all_gather | solution.py:75
  359.5 3.9 fusion.73
  363.4 36.5 %all-gather.28.cloned.1.call-done = bf16[1280,1024]{1,0:T(8,128)(2,1)} async-done(((bf16[640,1024]{1,0:T(8,128)(2,1)}), bf16[1280,1024]{1,0:T(8,128)(2,1)}) %all-gather.28.cloned.1.call-update) | async-done | bytes 2621456 | tf_op jit(solution)/shard_map/all_gather | solution.py:111
  400.0 3.0 copy.60
  403.0 38.2 %all-gather.26.cloned.1.call-done = bf16[1280,1024]{1,0:T(8,128)(2,1)} async-done(((bf16[640,1024]{1,0:T(8,128)(2,1)}), bf16[1280,1024]{1,0:T(8,128)(2,1)}) %all-gather.26.cloned.1.call-update) | async-done | bytes 2621456 | tf_op jit(solution)/shard_map/all_gather | solution.py:112
  441.1 4.4 copy.58
  445.5 21.7 %fusion.93 = (f32[16,640]{1,0:T(8,128)S(1)}, f32[16,640,1280]{2,1,0:T(8,128)}) fusion(bf16[640,16,64]{0,2,1:T(8,128)(2,1)} %bitcast.285, bf16[1280,16,64]{0,2,1:T(8,128)(2,1)S(1)} %bitcast.279, pred[640,1280]{1,0:T(8,128)(4,1)S(1)} %and_or_fusion), kind=kOutput, calls=%fused_computation.153 | convolution fusion | flops 1717032960 | bytes 57221120 | tf_op jit(solution)/shard_map/while/body/eval_jaxpr/qhd,khd->hqk/dot_general | solution.py:117
  467.2 17.5 fusion
  484.7 19.4 %fusion.50 = bf16[16,64,640]{2,1,0:T(8,128)(2,1)S(1)} fusion(bf16[1280,16,64]{0,2,1:T(8,128)(2,1)S(1)} %bitcast.291, f32[16,640,1280]{2,1,0:T(8,128)} %get-tuple-element.90, f32[16,640]{1,0:T(8,128)S(1)} %fusion, f32[16,640]{1,0:T(8,128)S(1)} %get-tuple-element.89), kind=kOutput, calls=%fused_computation.97 | convolution fusion | flops 1717698560 | bytes 56442880 | tf_op jit(solution)/shard_map/while/body/eval_jaxpr/hqk,khd->qhd/dot_general | solution.py:137
  504.2 3.7 fusion.94
  509.8 32.4 %fusion.6 = (f32[640,4096]{1,0:T(8,128)}, f32[640,4096]{1,0:T(8,128)}) fusion(bf16[1024,4096]{1,0:T(8,128)(2,1)} %bitcast.20, f32[1024]{0:T(1024)S(1)} %bitcast.331, f32[640]{0:T(1024)S(1)} %fusion.78, f32[1,640,1024]{2,1,0:T(8,128)} %copy-done.6, f32[640]{0:T(1024)S(1)} %broadcast_multiply_fusion, f32[1024]{0:T(1024)S(1)} %bitcast.311), kind=kOutput, calls=%fused_computation.13 | convolution fusion | flops 5534515200 | bytes 31994880 | tf_op jit(solution)/shard_map/dot_general | solution.py:152
  542.2 18.4 %all-gather.24.cloned.1.call-done = bf16[4096,1024]{1,0:T(8,128)(2,1)} async-done(((bf16[256,1024]{1,0:T(8,128)(2,1)}), bf16[4096,1024]{1,0:T(8,128)(2,1)}) %all-gather.24.cloned.1.call-update) | async-done | bytes 8388624 | tf_op jit(solution)/shard_map/all_gather | solution.py:73
  560.6 16.8 add_convert_fusion
  577.4 10.2 fusion.95
  587.6 2.1 fusion.46
  595.8 38.6 %multiply_reduce_fusion = (f32[16,640]{1,0:T(8,128)S(1)}, f32[16,640,1280]{2,1,0:T(8,128)}) fusion(f32[16,640,1280]{2,1,0:T(8,128)} %get-tuple-element.90, f32[16,640]{1,0:T(8,128)S(1)} %log_add_fusion, bf16[640,16,64]{0,2,1:T(8,128)(2,1)S(1)} %bitcast.288, bf16[1280,16,64]{0,2,1:T(8,128)(2,1)} %bitcast.290), kind=kOutput, calls=%fused_computation.1 | convolution fusion | flops 1717032960 | bytes 108871680 | tf_op jit(solution)/shard_map/while/body/eval_jaxpr/qhd,khd->hqk/dot_general | solution.py:181
  634.4 42.2 %multiply_convert_fusion = bf16[16,640,1280]{2,1,0:T(8,128)(2,1)} fusion(f32[16,640,1280]{2,1,0:T(8,128)} %get-tuple-element.96, f32[16,640,1280]{2,1,0:T(8,128)} %get-tuple-element.90, f32[16,640]{1,0:T(8,128)S(1)} %get-tuple-element.95, f32[16,640]{1,0:T(8,128)S(1)} %log_add_fusion), kind=kLoop, calls=%fused_computation | loop fusion | flops 52428800 | bytes 131153920 | tf_op jit(solution)/shard_map/while/body/eval_jaxpr/convert_element_type | solution.py:185
  676.6 14.6 multiply_convert_fusion.5
  691.2 4.5 copy.62
  695.8 21.4 %fusion.36 = bf16[16,64,1280]{2,1,0:T(8,128)(2,1)} fusion(bf16[640,16,64]{0,2,1:T(8,128)(2,1)S(1)} %bitcast.289, f32[16,640,1280]{2,1,0:T(8,128)} %get-tuple-element.90, f32[16,640]{1,0:T(8,128)S(1)} %log_add_fusion), kind=kOutput, calls=%fused_computation.67 | convolution fusion | flops 1705246720 | bytes 56401920 | tf_op jit(solution)/shard_map/while/body/eval_jaxpr/hqk,qhd->khd/dot_general | solution.py:211
  717.2 4.5 copy.63
  721.9 5.7 fusion.69
  727.6 14.9 multiply_convert_fusion.6
  742.4 5.2 fusion.96
  747.6 4.4 fusion.56
  752.0 19.7 %reduce-scatter.25.cloned.1.call-done = bf16[1,640,1024]{2,1,0:T(8,128)(2,1)} async-done(((bf16[1,1280,1024]{2,1,0:T(8,128)(2,1)}), bf16[1,640,1024]{2,1,0:T(8,128)(2,1)}) %reduce-scatter.25.cloned.1.call-update) | async-done | bytes 1310736 | tf_op jit(solution)/shard_map/reduce_scatter | solution.py:230
  771.7 5.9 fusion.45
  778.3 2.5 fusion.43
  780.7 5.5 fusion.71
  787.7 3.5 convert_bitcast_fusion.2
  792.8 4.5 fusion.90
  810.4 6.5 multiply_convert_fusion.2
  818.9 11.5 convert_bitcast_fusion.1
  830.4 7.8 copy.71
  838.3 24.6 %fusion.9 = bf16[4096,640]{0,1:T(8,128)(2,1)} fusion(f32[640,4096]{1,0:T(8,128)} %get-tuple-element.94), kind=kLoop, calls=%fused_computation.16 | loop fusion | flops 170393600 | bytes 15728640 | tf_op jit(solution)/shard_map/convert_element_type | solution.py:154
  862.9 7.9 copy.83
  870.8 11.5 convert_bitcast_fusion
  882.4 8.2 copy.73
  893.7 5.5 reduce-scatter.27.cloned.1.call-done
  899.3 34.0 %reduce-scatter.31.cloned.1.call-done = bf16[512,1024]{1,0:T(8,128)(2,1)} async-done(((bf16[1024,1024]{1,0:T(8,128)(2,1)}), bf16[512,1024]{1,0:T(8,128)(2,1)}) %reduce-scatter.31.cloned.1.call-update) | async-done | bytes 1048592 | tf_op jit(solution)/shard_map/reduce_scatter | solution.py:273
  933.4 56.4 %reduce-scatter.55.cloned.1.call-done = bf16[512,2048]{1,0:T(8,128)(2,1)} async-done(((bf16[1024,2048]{1,0:T(8,128)(2,1)}), bf16[512,2048]{1,0:T(8,128)(2,1)}) %reduce-scatter.55.cloned.1.call-update) | async-done | bytes 2097168 | tf_op jit(solution)/shard_map/reduce_scatter | solution.py:291
  989.9 56.5 %reduce-scatter.51.cloned.1.call-done = bf16[512,2048]{1,0:T(8,128)(2,1)} async-done(((bf16[1024,2048]{1,0:T(8,128)(2,1)}), bf16[512,2048]{1,0:T(8,128)(2,1)}) %reduce-scatter.51.cloned.1.call-update) | async-done | bytes 2097168 | tf_op jit(solution)/shard_map/reduce_scatter | solution.py:288
  1046.4 101.5 %reduce-scatter.43.cloned.1.call-done = bf16[512,4096]{1,0:T(8,128)(2,1)} async-done(((bf16[1024,4096]{1,0:T(8,128)(2,1)}), bf16[512,4096]{1,0:T(8,128)(2,1)}) %reduce-scatter.43.cloned.1.call-update) | async-done | bytes 4194320 | tf_op jit(solution)/shard_map/reduce_scatter | solution.py:282
  1148.2 101.2 %reduce-scatter.47.cloned.1.call-done = bf16[2048,1024]{1,0:T(8,128)(2,1)} async-done(((bf16[4096,1024]{1,0:T(8,128)(2,1)}), bf16[2048,1024]{1,0:T(8,128)(2,1)}) %reduce-scatter.47.cloned.1.call-update) | async-done | bytes 4194320 | tf_op jit(solution)/shard_map/reduce_scatter | solution.py:285
  1249.5 13.2 fusion.48
  1262.6 45.9 %reduce-scatter.61.cloned.1.call-done = bf16[32,8]{1,0:T(8,128)(2,1)} async-done(((bf16[512,8]{1,0:T(8,128)(2,1)}), bf16[32,8]{1,0:T(8,128)(2,1)}) %reduce-scatter.61.cloned.1.call-update) | async-done | bytes 528
  1309.9 58.7 %reduce-scatter.41.cloned.1.call-done = bf16[32,1024]{1,0:T(8,128)(2,1)} async-done(((bf16[512,1024]{1,0:T(8,128)(2,1)}), bf16[32,1024]{1,0:T(8,128)(2,1)}) %reduce-scatter.41.cloned.1.call-update) | async-done | bytes 65552 | tf_op jit(solution)/shard_map/reduce_scatter | solution.py:318
  1370.2 59.0 %reduce-scatter.37.cloned.1.call-done = bf16[32,1024]{1,0:T(8,128)(2,1)} async-done(((bf16[512,1024]{1,0:T(8,128)(2,1)}), bf16[32,1024]{1,0:T(8,128)(2,1)}) %reduce-scatter.37.cloned.1.call-update) | async-done | bytes 65552 | tf_op jit(solution)/shard_map/reduce_scatter | solution.py:315
  1430.7 58.5 %reduce-scatter.29.cloned.1.call-done = bf16[32,1024]{1,0:T(8,128)(2,1)} async-done(((bf16[512,1024]{1,0:T(8,128)(2,1)}), bf16[32,1024]{1,0:T(8,128)(2,1)}) %reduce-scatter.29.cloned.1.call-update) | async-done | bytes 65552 | tf_op jit(solution)/shard_map/reduce_scatter | solution.py:309
  1490.7 59.0 %reduce-scatter.33.cloned.1.call-done = bf16[32,1024]{1,0:T(8,128)(2,1)} async-done(((bf16[512,1024]{1,0:T(8,128)(2,1)}), bf16[32,1024]{1,0:T(8,128)(2,1)}) %reduce-scatter.33.cloned.1.call-update) | async-done | bytes 65552 | tf_op jit(solution)/shard_map/reduce_scatter | solution.py:312
  1551.2 62.7 %reduce-scatter.57.cloned.1.call-done = bf16[32,2048]{1,0:T(8,128)(2,1)} async-done(((bf16[512,2048]{1,0:T(8,128)(2,1)}), bf16[32,2048]{1,0:T(8,128)(2,1)}) %reduce-scatter.57.cloned.1.call-update) | async-done | bytes 131088 | tf_op jit(solution)/shard_map/reduce_scatter | solution.py:330
  1615.5 63.0 %reduce-scatter.53.cloned.1.call-done = bf16[32,2048]{1,0:T(8,128)(2,1)} async-done(((bf16[512,2048]{1,0:T(8,128)(2,1)}), bf16[32,2048]{1,0:T(8,128)(2,1)}) %reduce-scatter.53.cloned.1.call-update) | async-done | bytes 131088 | tf_op jit(solution)/shard_map/reduce_scatter | solution.py:327
  1680.1 73.8 %reduce-scatter.45.cloned.1.call-done = bf16[32,4096]{1,0:T(8,128)(2,1)} async-done(((bf16[512,4096]{1,0:T(8,128)(2,1)}), bf16[32,4096]{1,0:T(8,128)(2,1)}) %reduce-scatter.45.cloned.1.call-update) | async-done | bytes 262160 | tf_op jit(solution)/shard_map/reduce_scatter | solution.py:321
  1755.6 74.1 %reduce-scatter.49.cloned.1.call-done = bf16[128,1024]{1,0:T(8,128)(2,1)} async-done(((bf16[2048,1024]{1,0:T(8,128)(2,1)}), bf16[128,1024]{1,0:T(8,128)(2,1)}) %reduce-scatter.49.cloned.1.call-update) | async-done | bytes 262160 | tf_op jit(solution)/shard_map/reduce_scatter | solution.py:324
  (188 shorter events, 53.8 us)
Async XLA Ops:
  7.2 6.2 copy-start
  7.2 5.7 copy-start.4
  7.2 56.3 %all-gather.12.cloned.1.call-start = ((), (), s32[]{:S(2)}) async-start(), calls=%async_computation.21 | async-start | bytes 4456448 | tf_op jit(solution)/shard_map/all_gather | solution.py:74
  7.9 97.6 %all-gather.18.cloned.1.call-start = ((), (), s32[]{:S(2)}) async-start(), calls=%async_computation.24 | async-start | bytes 2228224 | tf_op jit(solution)/shard_map/all_gather | solution.py:67
  8.7 139.3 %all-gather.14.cloned.1.call-start = ((), (), s32[]{:S(2)}) async-start(), calls=%async_computation.22 | async-start | bytes 2228224 | tf_op jit(solution)/shard_map/all_gather | solution.py:68
  9.4 281.3 %all-gather.16.cloned.1.call-start = ((), (), s32[]{:S(2)}) async-start(), calls=%async_computation.23 | async-start | bytes 2228224 | tf_op jit(solution)/shard_map/all_gather | solution.py:66
  10.0 349.5 %all-gather.22.cloned.1.call-start = ((), (), s32[]{:S(2)}) async-start(), calls=%async_computation.26 | async-start | bytes 4456448 | tf_op jit(solution)/shard_map/all_gather | solution.py:75
  10.6 389.4 %all-gather.28.cloned.1.call-start = ((), (), s32[]{:S(2)}) async-start(), calls=%async_computation.48 | async-start | bytes 3932160 | tf_op jit(solution)/shard_map/all_gather | solution.py:111
  12.9 277.9 %copy-start.19 = (f32[640]{0:T(1024)}, f32[640]{0:T(1024)S(1)}, u32[]{:S(2)}) copy-start(f32[640]{0:T(1024)S(1)} %broadcast_multiply_fusion.1) | copy-start | bytes 7684
  13.3 96.5 %copy-start.27 = (f32[640]{0:T(1024)}, f32[640]{0:T(1024)S(1)}, u32[]{:S(2)}) copy-start(f32[640]{0:T(1024)S(1)} %fusion.44) | copy-start | bytes 7684
  13.4 277.4 %copy-start.23 = (f32[640]{0:T(1024)}, f32[640]{0:T(1024)S(1)}, u32[]{:S(2)}) copy-start(f32[640]{0:T(1024)S(1)} %fusion.77) | copy-start | bytes 7684
  13.5 346.0 %copy-start.25 = (f32[1,1024]{1,0:T(1,128)}, f32[1,1024]{1,0:T(1,128)S(1)}, u32[]{:S(2)}) copy-start(f32[1,1024]{1,0:T(1,128)S(1)} %fusion.79) | copy-start | bytes 12292
  67.4 223.3 %copy-start.21 = (f32[1,1024]{1,0:T(1,128)}, f32[1,1024]{1,0:T(1,128)S(1)}, u32[]{:S(2)}) copy-start(f32[1,1024]{1,0:T(1,128)S(1)} %get-tuple-element.87) | copy-start | bytes 12292
  67.4 223.3 %copy-start.29 = (f32[1,1024]{1,0:T(1,128)}, f32[1,1024]{1,0:T(1,128)S(1)}, u32[]{:S(2)}) copy-start(f32[1,1024]{1,0:T(1,128)S(1)} %get-tuple-element.88) | copy-start | bytes 12292
  109.8 43.1 %copy-start.18 = (bf16[64,4096]{1,0:T(8,128)(2,1)S(1)}, bf16[64,4096]{1,0:T(8,128)(2,1)}, u32[]{:S(2)}) copy-start(bf16[64,4096]{1,0:T(8,128)(2,1)} %param.22) | copy-start | bytes 1572868
  109.8 331.3 %all-gather.26.cloned.1.call-start = ((), (), s32[]{:S(2)}) async-start(), calls=%async_computation.47 | async-start | bytes 3932160 | tf_op jit(solution)/shard_map/all_gather | solution.py:112
  152.2 352.0 %all-gather.20.cloned.1.call-start = ((), (), s32[]{:S(2)}) async-start(), calls=%async_computation.25 | async-start | bytes 2228224 | tf_op jit(solution)/shard_map/all_gather | solution.py:69
  157.3 352.5 %all-to-all-start = ((bf16[16,64,4096]{2,1,0:T(8,128)(2,1)}), bf16[16,64,4096]{2,1,0:T(8,128)(2,1)}, u32[]{:S(2)}, u32[]{:S(2)}) async-start(bf16[16,64,4096]{2,1,0:T(8,128)(2,1)} %stack.2), calls=%async_computation | async-start | bytes 16777216 | tf_op jit(solution)/shard_map/all_to_all | solution.py:71
  162.0 398.6 %all-gather.24.cloned.1.call-start = ((), (), s32[]{:S(2)}) async-start(), calls=%async_computation.27 | async-start | bytes 8912896 | tf_op jit(solution)/shard_map/all_gather | solution.py:73
  162.7 584.9 %reduce-scatter.23.cloned.1.call-start = ((), (), s32[]{:S(2)}) async-start(), calls=%async_computation.28 | async-start | bytes 3932160 | tf_op jit(solution)/shard_map/reduce_scatter | solution.py:227
  402.9 42.6 %copy-start.2 = (bf16[1280,1024]{0,1:T(8,128)(2,1)}, bf16[1280,1024]{0,1:T(8,128)(2,1)S(1)}, u32[]{:S(2)}) copy-start(bf16[1280,1024]{0,1:T(8,128)(2,1)S(1)} %copy.60) | copy-start | bytes 7864324
  467.2 17.5 copy-start.11
  484.7 19.4 %copy-start.5 = (bf16[1,640,1024]{2,1,0:T(8,128)(2,1)S(1)}, bf16[1,640,1024]{2,1,0:T(8,128)(2,1)}, u32[]{:S(2)}) copy-start(bf16[1,640,1024]{2,1,0:T(8,128)(2,1)} %param.13) | copy-start | bytes 3932164
  504.1 3.7 copy-start.34
  507.9 1.5 copy-start.6
  509.8 50.8 %copy-start.13 = (bf16[1,640,1024]{2,1,0:T(8,128)(2,1)S(1)}, bf16[1,640,1024]{2,1,0:T(8,128)(2,1)}, u32[]{:S(2)}) copy-start(bf16[1,640,1024]{2,1,0:T(8,128)(2,1)} %param.14) | copy-start | bytes 3932164
  577.4 10.2 copy-start.7
  590.7 1.5 copy-start.9
  590.7 2.8 copy-start.32
  592.1 1.1 copy-start.17
  634.4 42.2 %copy-start.10 = (bf16[640,1024]{0,1:T(8,128)(2,1)S(1)}, bf16[640,1024]{0,1:T(8,128)(2,1)}, u32[]{:S(2)}) copy-start(bf16[640,1024]{0,1:T(8,128)(2,1)} %copy.59) | copy-start | bytes 3932164
  695.8 76.0 %reduce-scatter.25.cloned.1.call-start = ((), (), s32[]{:S(2)}) async-start(), calls=%async_computation.29 | async-start | bytes 3932160 | tf_op jit(solution)/shard_map/reduce_scatter | solution.py:230
  721.8 5.8 copy-start.3
  721.8 168.9 %reduce-scatter.59.cloned.1.call-start = ((), (), s32[]{:S(2)}) async-start(), calls=%async_computation.46 | async-start | bytes 24576 | tf_op jit(solution)/shard_map/reduce_scatter | solution.py:294
  742.4 5.2 copy-start.31
  747.6 24.1 %copy-start.20 = (f32[640]{0:T(1024)S(1)}, f32[640]{0:T(1024)}, u32[]{:S(2)}) copy-start(f32[640]{0:T(1024)} %copy-done.19) | copy-start | bytes 7684
  747.6 24.1 %copy-start.22 = (f32[1,1024]{1,0:T(1,128)S(1)}, f32[1,1024]{1,0:T(1,128)}, u32[]{:S(2)}) copy-start(f32[1,1024]{1,0:T(1,128)} %copy-done.21) | copy-start | bytes 12292
  752.0 25.5 %copy-start.28 = (f32[640]{0:T(1024)S(1)}, f32[640]{0:T(1024)}, u32[]{:S(2)}) copy-start(f32[640]{0:T(1024)} %copy-done.27) | copy-start | bytes 7684
  787.2 105.0 %reduce-scatter.39.cloned.1.call-start = ((), (), s32[]{:S(2)}) async-start(), calls=%async_computation.36 | async-start | bytes 3145728 | tf_op jit(solution)/shard_map/reduce_scatter | solution.py:279
  791.2 1.6 copy-start.30
  792.8 100.3 %reduce-scatter.35.cloned.1.call-start = ((), (), s32[]{:S(2)}) async-start(), calls=%async_computation.34 | async-start | bytes 3145728 | tf_op jit(solution)/shard_map/reduce_scatter | solution.py:276
  797.4 1.8 copy-start.16
  801.0 1.8 copy-start.15
  802.5 96.7 %reduce-scatter.27.cloned.1.call-start = ((), (), s32[]{:S(2)}) async-start(), calls=%async_computation.30 | async-start | bytes 3145728 | tf_op jit(solution)/shard_map/reduce_scatter | solution.py:270
  804.6 2.2 copy-start.33
  806.1 127.2 %reduce-scatter.31.cloned.1.call-start = ((), (), s32[]{:S(2)}) async-start(), calls=%async_computation.32 | async-start | bytes 3145728 | tf_op jit(solution)/shard_map/reduce_scatter | solution.py:273
  808.7 1.6 copy-start.26
  810.2 179.5 %reduce-scatter.55.cloned.1.call-start = ((), (), s32[]{:S(2)}) async-start(), calls=%async_computation.44 | async-start | bytes 6291456 | tf_op jit(solution)/shard_map/reduce_scatter | solution.py:291
  816.9 1.3 copy-start.12
  816.9 229.4 %reduce-scatter.51.cloned.1.call-start = ((), (), s32[]{:S(2)}) async-start(), calls=%async_computation.42 | async-start | bytes 6291456 | tf_op jit(solution)/shard_map/reduce_scatter | solution.py:288
  817.5 330.4 %reduce-scatter.43.cloned.1.call-start = ((), (), s32[]{:S(2)}) async-start(), calls=%async_computation.38 | async-start | bytes 12582912 | tf_op jit(solution)/shard_map/reduce_scatter | solution.py:282
  838.3 411.2 %reduce-scatter.47.cloned.1.call-start = ((), (), s32[]{:S(2)}) async-start(), calls=%async_computation.40 | async-start | bytes 12582912 | tf_op jit(solution)/shard_map/reduce_scatter | solution.py:285
  862.9 7.9 copy-start.14
  890.6 418.0 %reduce-scatter.61.cloned.1.call-start = ((), (), s32[]{:S(2)}) async-start(), calls=%async_computation.49 | async-start | bytes 139264
  892.2 476.5 %reduce-scatter.41.cloned.1.call-start = ((), (), s32[]{:S(2)}) async-start(), calls=%async_computation.37 | async-start | bytes 1114112 | tf_op jit(solution)/shard_map/reduce_scatter | solution.py:318
  892.9 536.2 %reduce-scatter.37.cloned.1.call-start = ((), (), s32[]{:S(2)}) async-start(), calls=%async_computation.35 | async-start | bytes 1114112 | tf_op jit(solution)/shard_map/reduce_scatter | solution.py:315
  893.7 595.5 %reduce-scatter.29.cloned.1.call-start = ((), (), s32[]{:S(2)}) async-start(), calls=%async_computation.31 | async-start | bytes 1114112 | tf_op jit(solution)/shard_map/reduce_scatter | solution.py:309
  899.3 650.4 %reduce-scatter.33.cloned.1.call-start = ((), (), s32[]{:S(2)}) async-start(), calls=%async_computation.33 | async-start | bytes 1114112 | tf_op jit(solution)/shard_map/reduce_scatter | solution.py:312
  933.3 680.5 %reduce-scatter.57.cloned.1.call-start = ((), (), s32[]{:S(2)}) async-start(), calls=%async_computation.45 | async-start | bytes 2228224 | tf_op jit(solution)/shard_map/reduce_scatter | solution.py:330
  989.8 688.6 %reduce-scatter.53.cloned.1.call-start = ((), (), s32[]{:S(2)}) async-start(), calls=%async_computation.43 | async-start | bytes 2228224 | tf_op jit(solution)/shard_map/reduce_scatter | solution.py:327
  1046.4 707.4 %reduce-scatter.45.cloned.1.call-start = ((), (), s32[]{:S(2)}) async-start(), calls=%async_computation.39 | async-start | bytes 4456448 | tf_op jit(solution)/shard_map/reduce_scatter | solution.py:321
  1148.0 101.5 %copy-start.8 = (f32[1,640,1024]{2,1,0:T(8,128)S(1)}, f32[1,640,1024]{2,1,0:T(8,128)}, u32[]{:S(2)}) copy-start(f32[1,640,1024]{2,1,0:T(8,128)} %copy-done.6) | copy-start | bytes 7864324
  1148.0 681.7 %reduce-scatter.49.cloned.1.call-start = ((), (), s32[]{:S(2)}) async-start(), calls=%async_computation.41 | async-start | bytes 4456448 | tf_op jit(solution)/shard_map/reduce_scatter | solution.py:324
  1249.5 582.0 %copy-start.1 = (bf16[8,1024]{1,0:T(8,128)(2,1)S(1)}, bf16[8,1024]{1,0:T(8,128)(2,1)}, u32[]{:S(2)}) copy-start(bf16[8,1024]{1,0:T(8,128)(2,1)} %param.17) | copy-start | bytes 49156
  (1 other events, 0.7 us)
Sparse Core Ops, SparseCore 0:
  10.2 53.2 all-gather.11
  65.7 39.8 all-gather.17
  107.7 40.1 all-gather.13
  150.0 140.7 all-gather.15
  292.8 66.6 all-gather.21
  361.5 38.4 all-gather.27
  402.1 39.0 all-gather.25
  443.3 41.3 all-gather.19
  486.9 73.6 all-gather.23
  695.9 35.8 reduce-scatter.22
  734.1 37.5 reduce-scatter.24
  787.4 9.7 reduce-scatter.58
  799.4 31.8 reduce-scatter.38
  833.4 31.8 reduce-scatter.34
  867.4 31.8 reduce-scatter.26
  901.4 31.8 reduce-scatter.30
  935.4 54.3 reduce-scatter.54
  992.0 54.2 reduce-scatter.50
  1048.6 99.2 reduce-scatter.42
  1150.2 99.2 reduce-scatter.46
  1253.5 55.0 reduce-scatter.60
  1312.2 56.4 reduce-scatter.40
  1372.7 56.3 reduce-scatter.36
  1432.7 56.4 reduce-scatter.28
  1493.2 56.3 reduce-scatter.32
  1553.2 60.5 reduce-scatter.56
  1617.9 60.4 reduce-scatter.52
  1682.3 71.4 reduce-scatter.44
  1758.2 71.4 reduce-scatter.48
